TPU v7x, 256 devices: a whole 4x4x8 slice. The times are simulated.
256 devices in a mesh: feat: 64 (over z_lo, y, x), tgt: 4 (over z_hi, core).
Axes of the slice: x: 4, y: 4, z: 8 (z_hi: 2, z_lo: 4; z = z_hi * 4 + z_lo), core: 2. Of those that a mesh axis runs over, the one named last changes fastest.
Arguments:
- tokens: bfloat16 [192, 4096], P('feat'), may hold values from -6 to 6
- encoder_weight: bfloat16 [4096, 16384], P(None, 'feat'), may hold values from -0.09375 to 0.09375
- encoder_bias: float32 [16384], P('feat'), may hold values from -1 to 0.25
- decoder_weight: bfloat16 [4, 16384, 4096], P('tgt', 'feat'), may hold values from -0.046875 to 0.046875
- decoder_bias: float32 [4, 4096], P('tgt'), may hold values from -3 to 3
- targets: bfloat16 [4, 192, 4096], P('tgt', 'feat'), may hold values from -6 to 6
Outputs:
- encoder_grad: float32 [4096, 16384], P(None, ('feat', 'tgt'))
- encoder_bias_grad: float32 [16384], P(('feat', 'tgt'))
- decoder_grad: float32 [4, 16384, 4096], P('tgt', 'feat')
- decoder_bias_grad: float32 [4, 4096], P('tgt')
All inputs are finite; a program needn't handle non-finite values.
Results may differ from a plain program's by a relative error of at most 0.005.
Values may be sent and summed in bfloat16 or wider, within the bound.
No kernel may reach another device: no remote copies, remote signals or barrier semaphores. Data moves between devices by JAX's collectives and lax.ppermute only.
A program may use at most 64 MiB of HBM per device.

v0:
```python
import jax
import jax.numpy as jnp
from jax import lax
from jax.sharding import PartitionSpec as P


def body(tokens, encoder_weight, encoder_bias, decoder_weight, decoder_bias, targets):
    all_rows = lax.all_gather(tokens, "feat", axis=0, tiled=True)
    pre_act = jnp.dot(all_rows, encoder_weight, preferred_element_type=jnp.float32) + encoder_bias
    positive = jnp.maximum(pre_act, 0.0)
    feats = (positive**2).astype(jnp.bfloat16)
    weight = decoder_weight[0]
    bias = decoder_bias[0]
    target = targets[0]
    summed = lax.psum_scatter(
        jnp.dot(feats, weight, preferred_element_type=jnp.float32),
        "feat",
        scatter_dimension=0,
        tiled=True,
    )
    error_part = (summed + bias - target.astype(jnp.float32)).astype(jnp.bfloat16)
    recon_error = lax.all_gather(error_part, "feat", axis=0, tiled=True)
    decoder_grads = [
        lax.dot_general(
            feats, recon_error, (((0,), (0,)), ((), ())), preferred_element_type=jnp.float32
        )
    ]
    bias_grads = [jnp.sum(recon_error.astype(jnp.float32), axis=0)]
    back_grad = lax.dot_general(
        recon_error, weight, (((1,), (1,)), ((), ())), preferred_element_type=jnp.float32
    )
    quarter = pre_act.shape[1] // lax.axis_size("tgt")
    offset = lax.axis_index("tgt") * quarter
    share = lax.psum_scatter(back_grad, "tgt", scatter_dimension=1, tiled=True)
    slope_share = 2.0 * lax.dynamic_slice_in_dim(positive, offset, quarter, 1)
    act_grad = share * slope_share
    encoder_bias_grad = jnp.sum(act_grad, axis=0)
    pre_grad = act_grad.astype(jnp.bfloat16)
    encoder_grad = lax.dot_general(
        all_rows, pre_grad, (((0,), (0,)), ((), ())), preferred_element_type=jnp.float32
    )
    return (encoder_grad, encoder_bias_grad, jnp.stack(decoder_grads), jnp.stack(bias_grads))


def solution(mesh):
    return jax.shard_map(
        body,
        mesh=mesh,
        in_specs=(
            P("feat", None),
            P(None, "feat"),
            P("feat"),
            P("tgt", "feat", None),
            P("tgt", None),
            P("tgt", "feat", None),
        ),
        out_specs=(
            P(None, ("feat", "tgt")),
            P(("feat", "tgt")),
            P("tgt", "feat", None),
            P("tgt", None),
        ),
        check_vma=False,
    )
```

profile of v0, /device:TPU:1, one launch (start us, length us, event | category | flops | bytes accessed | tf_op | source)
XLA Modules:
  0.0 1493.3 jit_solution(6703649330818770816)
XLA Ops:
  7.2 0.0 copy-start
  7.2 0.0 copy-start.4
  7.2 0.0 all-gather.5.cloned.1.call-start
  7.2 0.7 all-gather.5.cloned.1.call-update
  7.9 0.0 all-reduce.3.cloned.1.call-start
  8.0 310.1 %all-gather.5.cloned.1.call-done = bf16[64,3,4096]{2,1,0:T(4,128)(2,1)} async-done(((bf16[1,3,4096]{2,1,0:T(4,128)(2,1)}), bf16[64,3,4096]{2,1,0:T(4,128)(2,1)}) %all-gather.5.cloned.1.call-update) | async-done | bytes 1572880 | tf_op jit(solution)/shard_map/all_gather | solution.py:8
  318.0 4.3 reshape.13
  322.3 0.0 copy-done.4
  322.3 2.6 fusion.7
  325.0 0.0 copy-done
  325.0 2.2 fusion.2
  327.2 0.0 copy-start.5
  327.2 0.0 copy-start.2
  327.2 0.0 copy-start.3
  327.2 0.0 all-reduce.3.cloned.1.call-update
  327.3 0.0 all-gather.7.cloned.1.call-start
  327.3 0.6 copy-done.5
  327.9 0.6 dynamic-slice
  329.1 716.0 %all-reduce.3.cloned.1.call-done = f32[192,4096]{1,0:T(8,128)} async-done(((f32[192,4096]{1,0:T(8,128)}), f32[192,4096]{1,0:T(8,128)}) %all-reduce.3.cloned.1.call-update) | async-done | bytes 3145744
  1045.2 0.0 copy-done.2
  1045.2 0.0 copy-done.3
  1045.2 1.6 fusion.10
  1046.8 0.0 all-gather.7.cloned.1.call-update
  1046.8 0.0 reduce-scatter.4.cloned.1.call-start
  1046.9 348.8 %all-gather.7.cloned.1.call-done = bf16[64,3,4096]{2,1,0:T(4,128)(2,1)} async-done(((bf16[1,3,4096]{2,1,0:T(4,128)(2,1)}), bf16[64,3,4096]{2,1,0:T(4,128)(2,1)}) %all-gather.7.cloned.1.call-update) | async-done | bytes 1572880 | tf_op jit(solution)/shard_map/all_gather | solution.py:22
  1395.7 4.3 reshape.15
  1399.9 2.8 fusion.4
  1402.8 0.0 reduce-scatter.4.cloned.1.call-update
  1402.8 0.0 copy-start.1
  1402.8 2.4 convert_reduce_fusion
  1405.2 0.0 copy-done.1
  1405.2 2.8 convolution_bitcast_fusion
  1407.9 74.3 %reduce-scatter.4.cloned.1.call-done = f32[64,192]{1,0:T(8,128)} async-done(((f32[256,192]{1,0:T(8,128)}), f32[64,192]{1,0:T(8,128)}) %reduce-scatter.4.cloned.1.call-update) | async-done | bytes 49168
  1482.3 0.9 copy.15
  1483.2 2.9 convolution_bitcast_fusion.1
  1486.1 0.6 fusion.11
Async XLA Ops:
  7.2 317.8 %copy-start = (bf16[1,256,4096]{2,1,0:T(8,128)(2,1)S(1)}, bf16[1,256,4096]{2,1,0:T(8,128)(2,1)}, u32[]{:S(2)}) copy-start(bf16[1,256,4096]{2,1,0:T(8,128)(2,1)} %param.9) | copy-start | bytes 6291460
  7.2 315.1 %copy-start.4 = (f32[256]{0:T(256)S(1)}, f32[256]{0:T(256)}, u32[]{:S(2)}) copy-start(f32[256]{0:T(256)} %param.8) | copy-start | bytes 3076
  7.2 310.8 %all-gather.5.cloned.1.call-start = ((), (), s32[]{:S(2)}) async-start(), calls=%async_computation.1 | async-start | bytes 2129920 | tf_op jit(solution)/shard_map/all_gather | solution.py:8
  7.9 1037.2 %all-reduce.3.cloned.1.call-start = ((), (), s32[]{:S(2)}) async-start(), calls=%async_computation.4 | async-start | bytes 6291456
  327.2 0.7 copy-start.5
  327.2 717.9 %copy-start.2 = (bf16[1,3,4096]{2,1,0:T(4,128)(2,1)S(1)}, bf16[1,3,4096]{2,1,0:T(4,128)(2,1)}, u32[]{:S(2)}) copy-start(bf16[1,3,4096]{2,1,0:T(4,128)(2,1)} %param.11) | copy-start | bytes 73732
  327.2 717.9 %copy-start.3 = (f32[1,4096]{1,0:T(1,128)S(1)}, f32[1,4096]{1,0:T(1,128)}, u32[]{:S(2)}) copy-start(f32[1,4096]{1,0:T(1,128)} %param.10) | copy-start | bytes 49156
  327.3 1068.4 %all-gather.7.cloned.1.call-start = ((), (), s32[]{:S(2)}) async-start(), calls=%async_computation.2 | async-start | bytes 2129920 | tf_op jit(solution)/shard_map/all_gather | solution.py:22
  1046.8 435.5 %reduce-scatter.4.cloned.1.call-start = ((), (), s32[]{:S(2)}) async-start(), calls=%async_computation.3 | async-start | bytes 327680
  1402.8 2.4 copy-start.1
Sparse Core Ops, SparseCore 0:
  9.8 308.1 all-gather.4
  327.4 717.7 all-reduce.2
  1047.7 347.9 all-gather.6
  1402.9 79.3 reduce-scatter.3
where the time goes:
time: 1490 us
  waiting for transfers between devices  1450 us (97%)
    unnamed x6, waiting for transfers between devices  791 us
    all_gather x1, waiting for transfers between devices, body(): recon_error = lax.all_gather(error_part, 'feat', axis=0, tiled=True)  349 us
    all_gather x1, waiting for transfers between devices, body(): all_rows = lax.all_gather(tokens, 'feat', axis=0, tiled=True)  310 us
  transfers between devices with their start and end apart: 4, of which 4 were waited for; matrix products, arithmetic and copies ran while one was open for 0% of the time, Pallas kernels for 0%

commit v1 on v0

--- a/solution.py
+++ b/solution.py
@@ -2,6 +2,13 @@
 import jax.numpy as jnp
 from jax import lax
 from jax.sharding import PartitionSpec as P
+
+
+def swapped_in(array, axis, dim):
+    size = lax.axis_size(axis)
+    shards = jnp.stack([array for _ in range(size)])
+    shards = lax.all_to_all(shards, axis, split_axis=0, concat_axis=0)
+    return jnp.concatenate(shards, axis=dim)
 
 
 def body(tokens, encoder_weight, encoder_bias, decoder_weight, decoder_bias, targets):
@@ -19,7 +26,7 @@
         tiled=True,
     )
     error_part = (summed + bias - target.astype(jnp.float32)).astype(jnp.bfloat16)
-    recon_error = lax.all_gather(error_part, "feat", axis=0, tiled=True)
+    recon_error = swapped_in(error_part, "feat", 0)
     decoder_grads = [
         lax.dot_general(
             feats, recon_error, (((0,), (0,)), ((), ())), preferred_element_type=jnp.float32

time: 1490 us -> 1190 us (0.80)
  waiting for transfers between devices: 1450 us -> 1130 us
    all_gather x1 -> x0, waiting for transfers between devices: 349 us -> none  [body(): recon_error = lax.all_gather(error_part, 'feat', axis=0, tiled=True)]
    all_to_all x0 -> x1, waiting for transfers between devices: none -> 28.6 us  [swapped_in(): shards = lax.all_to_all(shards, axis, split_axis=0, concat_axis=0)]
    unnamed x6 -> x5, waiting for transfers between devices: 791 us -> 790 us
  transfers between devices with their start and end apart: 4 -> 4, of which waited for: 4 -> 4; matrix products, arithmetic and copies ran while one was open for 0% -> 1% of each run, Pallas kernels for 0% -> 0%
where the time goes in v1:
time: 1190 us; the launch traced here: 1180 us
  waiting for transfers between devices  1130 us (95%)
  matrix products  14.8 us (1%)
  between operations  14.5 us (1%)
  local copies, waits for them, and re-layouts  13.1 us (1%)
    unnamed x5, waiting for transfers between devices  790 us
    all_gather x1, waiting for transfers between devices, body(): all_rows = lax.all_gather(tokens, 'feat', axis=0, tiled=True)  310 us
    all_to_all x1, waiting for transfers between devices, swapped_in(): shards = lax.all_to_all(shards, axis, split_axis=0, concat_axis=0)  28.6 us
  transfers between devices with their start and end apart: 4, of which 4 were waited for; matrix products, arithmetic and copies ran while one was open for 1% of the time, Pallas kernels for 0%

profile of v1, /device:TPU:1, one launch (start us, length us, event | category | flops | bytes accessed | tf_op | source)
XLA Modules:
  0.0 1184.8 jit_solution(12152591275575421934)
XLA Ops:
  7.2 0.0 copy-start
  7.2 0.0 copy-start.3
  7.2 0.0 all-gather.3.cloned.1.call-start
  7.2 0.7 all-gather.3.cloned.1.call-update
  7.9 0.0 all-reduce.3.cloned.1.call-start
  8.0 310.1 %all-gather.3.cloned.1.call-done = bf16[64,3,4096]{2,1,0:T(4,128)(2,1)} async-done(((bf16[1,3,4096]{2,1,0:T(4,128)(2,1)}), bf16[64,3,4096]{2,1,0:T(4,128)(2,1)}) %all-gather.3.cloned.1.call-update) | async-done | bytes 1572880 | tf_op jit(solution)/shard_map/all_gather | solution.py:15
  318.0 4.3 reshape.19
  322.3 0.0 copy-done.3
  322.3 2.6 fusion.7
  325.0 0.0 copy-done
  325.0 2.2 fusion.2
  327.2 0.0 copy-start.4
  327.2 0.0 copy-start.1
  327.2 0.0 copy-start.2
  327.2 0.0 all-reduce.3.cloned.1.call-update
  327.3 0.6 copy-done.4
  327.9 0.6 dynamic-slice
  329.2 716.0 %all-reduce.3.cloned.1.call-done = f32[192,4096]{1,0:T(8,128)} async-done(((f32[192,4096]{1,0:T(8,128)}), f32[192,4096]{1,0:T(8,128)}) %all-reduce.3.cloned.1.call-update) | async-done | bytes 3145744
  1045.2 0.0 copy-done.1
  1045.2 0.0 copy-done.2
  1045.2 1.0 fusion.8
  1046.2 2.3 stack.6
  1048.5 9.2 all-to-all-start
  1057.7 0.0 reduce-scatter.4.cloned.1.call-start
  1057.7 28.6 %all-to-all-done = bf16[64,3,4096]{2,1,0:T(4,128)(2,1)} async-done(((bf16[64,3,4096]{2,1,0:T(4,128)(2,1)}), bf16[64,3,4096]{2,1,0:T(4,128)(2,1)}, u32[]{:S(2)}, u32[]{:S(2)}) %all-to-all-start) | async-done | bytes 1572896 | tf_op jit(solution)/shard_map/all_to_all | solution.py:10
  1086.3 4.3 reshape.16
  1090.6 2.8 fusion.4
  1093.5 0.0 reduce-scatter.4.cloned.1.call-update
  1093.5 4.2 convolution_bitcast_fusion
  1097.6 3.1 convert_reduce_fusion
  1100.8 73.1 %reduce-scatter.4.cloned.1.call-done = f32[64,192]{1,0:T(8,128)} async-done(((f32[256,192]{1,0:T(8,128)}), f32[64,192]{1,0:T(8,128)}) %reduce-scatter.4.cloned.1.call-update) | async-done | bytes 49168
  1173.9 0.9 copy.15
  1174.8 2.9 convolution_bitcast_fusion.1
  1177.7 0.6 fusion.10
Async XLA Ops:
  7.2 317.8 %copy-start = (bf16[1,256,4096]{2,1,0:T(8,128)(2,1)S(1)}, bf16[1,256,4096]{2,1,0:T(8,128)(2,1)}, u32[]{:S(2)}) copy-start(bf16[1,256,4096]{2,1,0:T(8,128)(2,1)} %param.9) | copy-start | bytes 6291460
  7.2 315.1 %copy-start.3 = (f32[256]{0:T(256)S(1)}, f32[256]{0:T(256)}, u32[]{:S(2)}) copy-start(f32[256]{0:T(256)} %param.8) | copy-start | bytes 3076
  7.2 310.8 %all-gather.3.cloned.1.call-start = ((), (), s32[]{:S(2)}) async-start(), calls=%async_computation.2 | async-start | bytes 2129920 | tf_op jit(solution)/shard_map/all_gather | solution.py:15
  7.9 1037.3 %all-reduce.3.cloned.1.call-start = ((), (), s32[]{:S(2)}) async-start(), calls=%async_computation.4 | async-start | bytes 6291456
  327.2 0.7 copy-start.4
  327.2 717.9 %copy-start.1 = (bf16[1,3,4096]{2,1,0:T(4,128)(2,1)S(1)}, bf16[1,3,4096]{2,1,0:T(4,128)(2,1)}, u32[]{:S(2)}) copy-start(bf16[1,3,4096]{2,1,0:T(4,128)(2,1)} %param.11) | copy-start | bytes 73732
  327.2 717.9 %copy-start.2 = (f32[1,4096]{1,0:T(1,128)S(1)}, f32[1,4096]{1,0:T(1,128)}, u32[]{:S(2)}) copy-start(f32[1,4096]{1,0:T(1,128)} %param.10) | copy-start | bytes 49156
  1048.5 37.8 %all-to-all-start = ((bf16[64,3,4096]{2,1,0:T(4,128)(2,1)}), bf16[64,3,4096]{2,1,0:T(4,128)(2,1)}, u32[]{:S(2)}, u32[]{:S(2)}) async-start(bf16[64,3,4096]{2,1,0:T(4,128)(2,1)} %stack.6), calls=%async_computation | async-start | bytes 4194304 | tf_op jit(solution)/shard_map/all_to_all | solution.py:10
  1057.7 116.2 %reduce-scatter.4.cloned.1.call-start = ((), (), s32[]{:S(2)}) async-start(), calls=%async_computation.3 | async-start | bytes 327680
Sparse Core Ops, SparseCore 0:
  9.8 308.1 all-gather.2
  327.4 717.7 all-reduce.2
  1093.6 80.1 reduce-scatter.3
